TPU v7x, 32 devices: a whole 2x2x4 slice. The times are simulated.
32 devices in a mesh: group: 2 (over y), tile: 4 (over z), list: 4 (over x, core).
Axes of the slice: x: 2, y: 2, z: 4, core: 2. Of those that a mesh axis runs over, the one named last changes fastest.
Arguments:
- probes: float32 [8192, 256], P(('group', 'tile', 'list')), parts along dimension 0, may hold values from -6 to 6
- right_bases: bfloat16 [8, 1, 96, 1024], P(('group', 'tile'), None, 'list'), parts along dimension 0, may hold values from -0.1875 to 0.1875
- left_bases: bfloat16 [8, 1, 96, 1024], P(('group', 'tile'), None, 'list'), parts along dimension 0, may hold values from -0.625 to 0.625
- near_tiles: bfloat16 [8, 1024, 3, 1024], P(('group', 'tile'), None, None, 'list'), parts along dimension 0, may hold values from -0.109375 to 0.109375
- tile_ranks: int32 [8, 1], P(('group', 'tile')), parts along dimension 0, may hold values from 32 to 96
- column_rows: int32 [4, 1], P('tile'), may hold values from 0 to 3, as said below
- row_columns: int32 [4, 1], P('tile'), may hold values from 0 to 3, as said below
Outputs:
- product: float32 [8192, 256], P(('group', 'tile', 'list')), parts along dimension 0
There are 2 independent parts, one for each index of `group`. A program takes and returns all parts, laid end to end along the dimension named above; an argument that names none is the same for every part. Nothing has to cross between parts.
Inputs may be any that keep to these rules, and one draw needn't show every extreme that they name: `column_rows`: each row j lists 1 distinct tile rows. Tile (i, j) is listed in row j here exactly when j is listed in row i of row_columns. A listed tile may lie beside the diagonal; its low-rank term then adds to the dense tile. `row_columns`: each row i lists 1 distinct tile columns, matching column_rows.
All inputs are finite; a program needn't handle non-finite values.
Results may differ from a plain program's by a relative error of at most 0.0048.
Values may be sent and summed in bfloat16 or wider, within the bound.
A program may use at most 64 MiB of HBM per device.

v0:
```python
import functools

import jax
import jax.numpy as jnp
from jax import lax
from jax.experimental import pallas as pl
from jax.experimental.pallas import tpu as pltpu
from jax.sharding import PartitionSpec as P

MESH = pl.DeviceIdType.MESH
BF16 = jnp.bfloat16
F32 = jnp.float32
CHUNKS = 2
FLIPS = ((0, 0), (0, 1), (1, 0), (1, 1))


def fused_kernel(
    tiles, near, right, left, probes, ranks, rows, out,
    near_v, probe_v, right_v, left_v, right_x, left_x, right_c, left_t,
    w, zbuf, center, kept, osend, orecv, xsend, xrecv, fin,
    pc, prec, cbuf, crecv, sbuf, srecv,
    local_sem, set_send, set_recv, z_send, z_recv, p_send, p_recv,
    c_send, c_recv, s_send, s_recv, o_send, o_recv, x_send, x_recv,
):
    g, t, l = lax.axis_index("group"), lax.axis_index("tile"), lax.axis_index("list")
    x, c = l // 2, l % 2
    rank_part = right.shape[0]
    shard = probes.shape[0]
    width = probes.shape[1] // CHUNKS

    def peer(k):
        return (x + FLIPS[k][0]) % 2 * 2 + (c + FLIPS[k][1]) % 2

    loads = [pltpu.make_async_copy(probes, probe_v, local_sem.at[0])]
    for at, s in enumerate((1, 0, 2)):
        place = (2, 0, 1)[at]
        loads.append(
            pltpu.make_async_copy(
                near.at[s], near_v.at[:, :, pl.ds(place * shard, shard)], local_sem.at[1 + at]
            )
        )
    own = pl.ds(pl.multiple_of(l * shard, shard), shard)
    loads.insert(0, pltpu.make_async_copy(right, right_v, local_sem.at[4]))
    loads.insert(2, pltpu.make_async_copy(left, left_v, local_sem.at[5]))
    for load in loads:
        load.start()

    barrier = pltpu.get_barrier_semaphore()
    for k in (1, 2, 3):
        pl.semaphore_signal(barrier, inc=1, device_id=(g, t, peer(k)), device_id_type=MESH)
    for d in range(1, tiles):
        pl.semaphore_signal(barrier, inc=1, device_id=(g, (t + d) % tiles, l), device_id_type=MESH)

    @pl.when(t == 0)
    def _():
        zbuf[:, :, 0:shard, :] = jnp.zeros((2, CHUNKS, shard, width), BF16)

    @pl.when(t == tiles - 1)
    def _():
        zbuf[:, :, shard : 2 * shard, :] = jnp.zeros((2, CHUNKS, shard, width), BF16)

    loads[1].wait()
    for ch in range(CHUNKS):
        w[0, ch] = probe_v[:, ch * width : (ch + 1) * width].astype(BF16)
    pl.semaphore_wait(barrier, 3 + tiles - 1)

    sent = []

    def send(src, dst, ssem, rsem, tile, lst):
        copy = pltpu.make_async_remote_copy(
            src_ref=src, dst_ref=dst, send_sem=ssem, recv_sem=rsem,
            device_id=(g, tile, lst), device_id_type=MESH,
        )
        copy.start()
        sent.append(copy)
        return copy

    def z_copy(p, ch, way):
        return pltpu.make_async_remote_copy(
            src_ref=w.at[p, ch],
            dst_ref=zbuf.at[p, ch, pl.ds(way * shard, shard)],
            send_sem=z_send.at[p, ch, way],
            recv_sem=z_recv.at[p, ch, way],
            device_id=(g, (t + (1 if way == 0 else tiles - 1)) % tiles, l),
            device_id_type=MESH,
        )

    def z_start(p, ch):
        @pl.when(t < tiles - 1)
        def _():
            z_copy(p, ch, 0).start()

        @pl.when(t > 0)
        def _():
            z_copy(p, ch, 1).start()

    def z_wait(p, ch):
        @pl.when(t > 0)
        def _():
            z_copy(p, ch, 0).wait_recv()

        @pl.when(t < tiles - 1)
        def _():
            z_copy(p, ch, 1).wait_recv()

    order = [((x + 1) % 2) * 2 + (1 - c), x * 2 + (1 - c), ((x + 1) % 2) * 2 + c, x * 2 + c]
    flying = {}

    def stage_pc(p, ch):
        values = jnp.dot(right_c[...], w[p, ch], preferred_element_type=F32)
        for k in range(4):
            pc[p, ch, k] = values[k * rank_part : (k + 1) * rank_part].astype(BF16)
        for k in (1, 2, 3):
            flying["p", p, ch, k] = send(
                pc.at[p, ch, k], prec.at[p, ch, k - 1],
                p_send.at[p, ch, k - 1], p_recv.at[p, ch, k - 1], t, peer(k),
            )

    def stage_center(p, ch):
        for at in range(4):
            center[ch, at] = jnp.dot(
                near_v[order[at], :, 2 * shard : 3 * shard], w[p, ch], preferred_element_type=F32
            )

    def stage_b(p, ch):
        for k in (1, 2, 3):
            flying["p", p, ch, k].wait_recv()
        values = sum(prec[p, ch, k].astype(F32) for k in range(3)) + pc[p, ch, 0].astype(F32)
        level = l * rank_part + lax.broadcasted_iota(jnp.int32, values.shape, 0)
        cbuf[p, ch] = jnp.where(level < ranks[0, 0], values, 0.0).astype(BF16)
        for d in range(1, tiles):
            flying["c", p, ch, d] = send(
                cbuf.at[p, ch], crecv.at[p, ch, d - 1],
                c_send.at[p, ch, d - 1], c_recv.at[p, ch, d - 1], (t + d) % tiles, l,
            )

    def stage_c(p, ch):
        z_wait(p, ch)
        for at in range(4):
            value = center[ch, at] + jnp.dot(
                near_v[order[at], :, 0 : 2 * shard], zbuf[p, ch], preferred_element_type=F32
            )
            if at < 2:
                osend[p, ch, at] = value.astype(BF16)
                flying["o", p, ch, at] = send(
                    osend.at[p, ch, at], orecv.at[p, ch, at],
                    o_send.at[p, ch, at], o_recv.at[p, ch, at], t, peer(1),
                )
            else:
                kept[ch, at - 2] = value

    def stage_d(p, ch):
        flying["o", p, ch, 0].wait_recv()
        xsend[p, ch] = (kept[ch, 0] + orecv[p, ch, 0].astype(F32)).astype(BF16)
        flying["x", p, ch] = send(
            xsend.at[p, ch], xrecv.at[p, ch], x_send.at[p, ch], x_recv.at[p, ch], t, peer(2)
        )
        flying["o", p, ch, 1].wait_recv()
        fin[ch] = kept[ch, 1] + orecv[p, ch, 1].astype(F32)

    def stage_e(p, ch):
        wanted = rows[0, 0]
        chosen = jnp.where(wanted == t, cbuf[p, ch].astype(F32), 0.0)
        for d in range(1, tiles):
            flying["c", p, ch, d].wait_recv()
            source = (t + tiles - d) % tiles
            chosen = jnp.where(wanted == source, crecv[p, ch, d - 1].astype(F32), chosen)
        sbuf[p, ch] = chosen.astype(BF16)
        for k in (1, 2, 3):
            flying["s", p, ch, k] = send(
                sbuf.at[p, ch], srecv.at[p, ch, k - 1],
                s_send.at[p, ch, k - 1], s_recv.at[p, ch, k - 1], t, peer(k),
            )

    def stage_f(p, ch):
        parts = [sbuf[p, ch].astype(F32)]
        for k in (1, 2, 3):
            flying["s", p, ch, k].wait_recv()
            parts.append(srecv[p, ch, k - 1].astype(F32))
        coefficients = jnp.concatenate(parts, axis=0).astype(BF16)
        far = fin[ch] + jnp.dot(left_t[...], coefficients, preferred_element_type=F32)
        flying["x", p, ch].wait_recv()
        value = far + xrecv[p, ch].astype(F32)
        if p == 0:
            w[1, ch] = value.astype(BF16)
        else:
            out[:, ch * width : (ch + 1) * width] = value

    def bases(source, held, base):
        copies = []
        for k in (1, 2, 3):
            columns = pl.ds(pl.multiple_of(peer(k) * shard, shard), shard)
            copies.append(
                send(
                    source.at[:, columns], held.at[k],
                    set_send.at[base + k], set_recv.at[base + k], t, peer(k),
                )
            )
        return copies

    loads[0].wait()
    right_copies = bases(right_v, right_x, 0)
    for ch in range(CHUNKS):
        z_start(0, ch)
    loads[2].wait()
    left_copies = bases(left_v, left_x, 4)
    for copy in right_copies:
        copy.wait_recv()
    right_c[...] = jnp.concatenate([right_v[:, own].astype(F32)] + [right_x[k].astype(F32) for k in (1, 2, 3)], axis=0).astype(BF16)
    for ch in range(CHUNKS):
        stage_pc(0, ch)
    loads[3].wait()
    for ch in range(CHUNKS):
        stage_center(0, ch)
    loads[4].wait()
    loads[5].wait()

    for p in range(2):
        stage_b(p, 0)
        stage_c(p, 0)
        stage_b(p, 1)
        stage_c(p, 1)
        if p == 0:
            for copy in left_copies:
                copy.wait_recv()
            left_t[...] = (
                jnp.concatenate([left_v[:, own].astype(F32)] + [left_x[k].astype(F32) for k in (1, 2, 3)], axis=0).T.astype(BF16)
            )
        stage_d(p, 0)
        stage_e(p, 0)
        stage_d(p, 1)
        stage_e(p, 1)
        for ch in range(CHUNKS):
            stage_f(p, ch)
            if p == 0:
                z_start(1, ch)
                stage_pc(1, ch)
                stage_center(1, ch)

    for copy in sent:
        copy.wait_send()
    for p in range(2):
        for ch in range(CHUNKS):

            @pl.when(t < tiles - 1)
            def _():
                z_copy(p, ch, 0).wait_send()

            @pl.when(t > 0)
            def _():
                z_copy(p, ch, 1).wait_send()


def fused(tiles, probes, right_bases, left_bases, near_tiles, tile_ranks, row_columns):
    rank_part = right_bases.shape[2]
    shard, probe_count = probes.shape
    width = probe_count // CHUNKS
    near = near_tiles[0].transpose(1, 0, 2).reshape(3, 4, shard, shard)
    both = (2, CHUNKS)
    any_spec = pl.BlockSpec(memory_space=pltpu.HBM)
    smem_spec = pl.BlockSpec(memory_space=pltpu.SMEM)
    dma = pltpu.SemaphoreType.DMA
    return pl.pallas_call(
        functools.partial(fused_kernel, tiles),
        out_shape=jax.ShapeDtypeStruct((shard, probe_count), F32),
        in_specs=[any_spec] * 4 + [smem_spec] * 2,
        out_specs=pl.BlockSpec(memory_space=pltpu.VMEM),
        scratch_shapes=[
            pltpu.VMEM((4, shard, 3 * shard), BF16),
            pltpu.VMEM((shard, probe_count), F32),
            pltpu.VMEM((rank_part, 4 * shard), BF16),
            pltpu.VMEM((rank_part, 4 * shard), BF16),
            pltpu.VMEM((4, rank_part, shard), BF16),
            pltpu.VMEM((4, rank_part, shard), BF16),
            pltpu.VMEM((4 * rank_part, shard), BF16),
            pltpu.VMEM((shard, 4 * rank_part), BF16),
            pltpu.VMEM(both + (shard, width), BF16),
            pltpu.VMEM(both + (2 * shard, width), BF16),
            pltpu.VMEM((CHUNKS, 4, shard, width), F32),
            pltpu.VMEM((CHUNKS, 2, shard, width), F32),
            pltpu.VMEM(both + (2, shard, width), BF16),
            pltpu.VMEM(both + (2, shard, width), BF16),
            pltpu.VMEM(both + (shard, width), BF16),
            pltpu.VMEM(both + (shard, width), BF16),
            pltpu.VMEM((CHUNKS, shard, width), F32),
            pltpu.VMEM(both + (4, rank_part, width), BF16),
            pltpu.VMEM(both + (3, rank_part, width), BF16),
            pltpu.VMEM(both + (rank_part, width), BF16),
            pltpu.VMEM(both + (tiles - 1, rank_part, width), BF16),
            pltpu.VMEM(both + (rank_part, width), BF16),
            pltpu.VMEM(both + (3, rank_part, width), BF16),
            dma((6,)), dma((8,)), dma((8,)), dma(both + (2,)), dma(both + (2,)),
            dma(both + (3,)), dma(both + (3,)), dma(both + (tiles - 1,)), dma(both + (tiles - 1,)),
            dma(both + (3,)), dma(both + (3,)), dma(both + (2,)), dma(both + (2,)),
            dma(both), dma(both),
        ],
        compiler_params=pltpu.CompilerParams(
            collective_id=0, has_side_effects=True, vmem_limit_bytes=67_043_328
        ),
    )(near, right_bases[0, 0], left_bases[0, 0], probes, tile_ranks, row_columns)


def shifted(block, axis, distance):
    devices = range(lax.axis_size(axis))
    route = [(i - distance, i) for i in devices if i - distance in devices]
    return lax.ppermute(block, axis, route)


def image_part(operand, right_bases, left_bases, near_tiles, tile_ranks, column_rows, row_columns):
    tile_slots = right_bases.shape[1]
    rank_part = right_bases.shape[2]
    tile_rows = right_bases.shape[3]
    probe_count = operand.shape[1]
    tile_count = lax.axis_size("tile")
    right_flat = right_bases.reshape(tile_slots * rank_part, tile_rows)
    left_flat = left_bases.reshape(tile_slots * rank_part, tile_rows)
    dense_flat = near_tiles.reshape(tile_rows, -1)
    values = jnp.dot(
        right_flat,
        lax.all_gather(operand, "list", axis=0, tiled=True),
        preferred_element_type=jnp.float32,
    )
    rank_level = lax.axis_index("list") * rank_part + lax.iota(jnp.int32, rank_part)
    rank_mask = rank_level[None, :] < tile_ranks[0][:, None]
    coefficients = jnp.where(
        rank_mask[:, :, None], values.reshape(tile_slots, rank_part, probe_count), 0.0
    ).astype(jnp.bfloat16)
    targets = (column_rows[0][None, :] == lax.iota(jnp.int32, tile_count)[:, None]).astype(
        jnp.bfloat16
    )
    outgoing = jnp.einsum(
        "dk,krp->drp", targets, coefficients, preferred_element_type=jnp.float32
    ).astype(jnp.bfloat16)
    sources = (row_columns[0][:, None] == lax.iota(jnp.int32, tile_count)[None, :]).astype(
        jnp.bfloat16
    )
    chosen = jnp.einsum(
        "kj,jrp->krp",
        sources,
        lax.all_to_all(outgoing, "tile", split_axis=0, concat_axis=0, tiled=True),
        preferred_element_type=jnp.float32,
    ).astype(jnp.bfloat16)
    chosen = chosen.reshape(tile_slots * rank_part, -1)
    far_sum = lax.dot_general(
        left_flat, chosen, (((0,), (0,)), ((), ())), preferred_element_type=jnp.float32
    )
    arrived = {}
    for offset in (1, -1):
        arrived[offset] = shifted(operand, "tile", offset)
    stacked = jnp.concatenate([arrived[1], operand, arrived[-1]], axis=0)
    near_sum = jnp.dot(dense_flat, stacked, preferred_element_type=jnp.float32)
    partial_image = near_sum + far_sum
    return lax.psum_scatter(partial_image, "list", scatter_dimension=0, tiled=True)


def local(probes, right_bases, left_bases, near_tiles, tile_ranks, column_rows, row_columns):
    list_count, tile_count = lax.axis_size("list"), lax.axis_size("tile")
    if list_count == 4 and right_bases.shape[1] == 1 and 2 < tile_count <= 8:
        return fused(
            tile_count, probes, right_bases, left_bases, near_tiles, tile_ranks, row_columns
        )
    probe_bf = probes.astype(jnp.bfloat16)
    first_pass = image_part(
        probe_bf, right_bases, left_bases, near_tiles, tile_ranks, column_rows, row_columns
    ).astype(jnp.bfloat16)
    return image_part(
        first_pass, right_bases, left_bases, near_tiles, tile_ranks, column_rows, row_columns
    )


def solution(mesh):
    placed = (
        P(("group", "tile", "list"), None),
        P(("group", "tile"), None, "list", None),
        P(("group", "tile"), None, "list", None),
        P(("group", "tile"), None, None, "list"),
        P(("group", "tile"), None),
        P("tile", None),
        P("tile", None),
    )
    return jax.shard_map(
        local,
        mesh=mesh,
        in_specs=placed,
        out_specs=P(("group", "tile", "list"), None),
        check_vma=False,
    )
```

profile of v0, /device:TPU:0, one launch (start us, length us, event | category | flops | bytes accessed | tf_op | source)
XLA Modules:
  0.0 32.6 jit_solution(6968137394534321021)
XLA Ops:
  1.3 29.7 %shard_map.64 = f32[256,256]{1,0:T(8,128)} custom-call(bf16[3,4,256,256]{3,2,1,0:T(8,128)(2,1)} %bitcast.7, bf16[24,1024]{1,0:T(8,128)(2,1)} %bitcast.8, bf16[24,1024]{1,0:T(8,128)(2,1)} %bitcast.9, f32[256,256]{1,0:T(8,128)} %probes.1, s32[1,1]{1,0:T(1,128)S(6)} %copy.8.ranks, s32[1,1]{1,0:T(1,128)S(6)} %copy.9.rows), custom_call_target="tpu_custom_call" | custom-call | tf_op jit(solution)/shard_map/pallas_call | solution.py:263
  31.0 1.7 %copy.10 = f32[256,256]{1,0:T(8,128)} copy(f32[256,256]{1,0:T(8,128)} %shard_map.64) | data formatting | bytes 524288
where the time goes:
time: 32.8 us; the launch traced here: 32.6 us
  Pallas kernels  29.7 us (91%)
  local copies, waits for them, and re-layouts  1.67 us (5%)
  between operations  1.3 us (4%)
    pallas_call x1, Pallas kernels, fused(): pl.pallas_call(functools.partial(fused_kernel, tiles), out_shape=jax.Shap...  29.7 us
    unnamed x1, local copies, waits for them, and re-layouts  1.67 us

commit v1 on v0

--- a/solution.py
+++ b/solution.py
@@ -16,10 +16,11 @@
 
 def fused_kernel(
     tiles, near, right, left, probes, ranks, rows, out,
-    near_v, probe_v, right_v, left_v, right_x, left_x, right_c, left_t,
-    w, zbuf, center, kept, osend, orecv, xsend, xrecv, fin,
-    pc, prec, cbuf, crecv, sbuf, srecv,
-    local_sem, set_send, set_recv, z_send, z_recv, p_send, p_recv,
+    near_v, probe_v, right_v, left_v, right_x, left_x, left_n, right_c, left_t, left_tn,
+    row_send, row_recv, mix_part, mix_recv, mix,
+    w, zbuf, stack, center, kept, osend, orecv, xsend, xrecv, fin,
+    pc, prec, cbuf, crecv, sbuf, srecv, sbuf2, srecv2,
+    local_sem, set_send, set_recv, side_send, side_recv, z_send, z_recv, p_send, p_recv,
     c_send, c_recv, s_send, s_recv, o_send, o_recv, x_send, x_recv,
 ):
     g, t, l = lax.axis_index("group"), lax.axis_index("tile"), lax.axis_index("list")
@@ -27,9 +28,14 @@
     rank_part = right.shape[0]
     shard = probes.shape[0]
     width = probes.shape[1] // CHUNKS
+    padding = right_c.shape[0] - 4 * rank_part
 
     def peer(k):
         return (x + FLIPS[k][0]) % 2 * 2 + (c + FLIPS[k][1]) % 2
+
+    def joined(parts):
+        rest = [jnp.zeros((padding, parts[0].shape[1]), F32)] if padding else []
+        return jnp.concatenate([part.astype(F32) for part in parts] + rest, axis=0)
 
     loads = [pltpu.make_async_copy(probes, probe_v, local_sem.at[0])]
     for at, s in enumerate((1, 0, 2)):
@@ -51,13 +57,15 @@
     for d in range(1, tiles):
         pl.semaphore_signal(barrier, inc=1, device_id=(g, (t + d) % tiles, l), device_id_type=MESH)
 
-    @pl.when(t == 0)
-    def _():
-        zbuf[:, :, 0:shard, :] = jnp.zeros((2, CHUNKS, shard, width), BF16)
-
-    @pl.when(t == tiles - 1)
-    def _():
-        zbuf[:, :, shard : 2 * shard, :] = jnp.zeros((2, CHUNKS, shard, width), BF16)
+    for way, edge in ((0, 0), (1, tiles - 1)):
+
+        @pl.when(t == edge)
+        def _():
+            zbuf[:, :, way * shard : (way + 1) * shard, :] = jnp.zeros((2, CHUNKS, shard, width), BF16)
+            left_n[way] = jnp.zeros(left_n.shape[1:], BF16)
+            row_recv[way] = jnp.full(row_recv.shape[1:], -1, jnp.int32)
+
+    row_send[...] = jnp.full(row_send.shape, rows[0, 0], jnp.int32)
 
     loads[1].wait()
     for ch in range(CHUNKS):
@@ -75,36 +83,44 @@
         sent.append(copy)
         return copy
 
-    def z_copy(p, ch, way):
-        return pltpu.make_async_remote_copy(
-            src_ref=w.at[p, ch],
-            dst_ref=zbuf.at[p, ch, pl.ds(way * shard, shard)],
-            send_sem=z_send.at[p, ch, way],
-            recv_sem=z_recv.at[p, ch, way],
-            device_id=(g, (t + (1 if way == 0 else tiles - 1)) % tiles, l),
-            device_id_type=MESH,
-        )
+    class Both:
+        def __init__(self, src, dst, ssem, rsem):
+            self.copies = [
+                pltpu.make_async_remote_copy(
+                    src_ref=src, dst_ref=dst(way), send_sem=ssem.at[way], recv_sem=rsem.at[way],
+                    device_id=(g, (t + (1 if way == 0 else tiles - 1)) % tiles, l),
+                    device_id_type=MESH,
+                )
+                for way in range(2)
+            ]
+
+        def each(self, act, holds):
+            for copy, held in zip(self.copies, holds):
+
+                @pl.when(held)
+                def _(copy=copy):
+                    act(copy)
+
+        def start(self):
+            self.each(lambda copy: copy.start(), (t < tiles - 1, t > 0))
+            return self
+
+        def wait_send(self):
+            self.each(lambda copy: copy.wait_send(), (t < tiles - 1, t > 0))
+
+        def wait_recv(self):
+            self.each(lambda copy: copy.wait_recv(), (t > 0, t < tiles - 1))
+
+    flying = {}
 
     def z_start(p, ch):
-        @pl.when(t < tiles - 1)
-        def _():
-            z_copy(p, ch, 0).start()
-
-        @pl.when(t > 0)
-        def _():
-            z_copy(p, ch, 1).start()
-
-    def z_wait(p, ch):
-        @pl.when(t > 0)
-        def _():
-            z_copy(p, ch, 0).wait_recv()
-
-        @pl.when(t < tiles - 1)
-        def _():
-            z_copy(p, ch, 1).wait_recv()
+        flying["z", p, ch] = Both(
+            w.at[p, ch], lambda way: zbuf.at[p, ch, pl.ds(way * shard, shard)],
+            z_send.at[p, ch], z_recv.at[p, ch],
+        ).start()
+        sent.append(flying["z", p, ch])
 
     order = [((x + 1) % 2) * 2 + (1 - c), x * 2 + (1 - c), ((x + 1) % 2) * 2 + c, x * 2 + c]
-    flying = {}
 
     def stage_pc(p, ch):
         values = jnp.dot(right_c[...], w[p, ch], preferred_element_type=F32)
@@ -112,20 +128,22 @@
             pc[p, ch, k] = values[k * rank_part : (k + 1) * rank_part].astype(BF16)
         for k in (1, 2, 3):
             flying["p", p, ch, k] = send(
-                pc.at[p, ch, k], prec.at[p, ch, k - 1],
+                pc.at[p, ch, peer(k)], prec.at[p, ch, k - 1],
                 p_send.at[p, ch, k - 1], p_recv.at[p, ch, k - 1], t, peer(k),
             )
 
-    def stage_center(p, ch):
+    def stage_center(ch):
         for at in range(4):
             center[ch, at] = jnp.dot(
-                near_v[order[at], :, 2 * shard : 3 * shard], w[p, ch], preferred_element_type=F32
-            )
-
-    def stage_b(p, ch):
+                near_v[order[at], :, 2 * shard : 3 * shard], w[0, ch], preferred_element_type=F32
+            )
+
+    def stage_b(p, ch, more=None):
         for k in (1, 2, 3):
             flying["p", p, ch, k].wait_recv()
-        values = sum(prec[p, ch, k].astype(F32) for k in range(3)) + pc[p, ch, 0].astype(F32)
+        values = sum(prec[p, ch, k].astype(F32) for k in range(3)) + pc[p, ch, l].astype(F32)
+        if more is not None:
+            values = values + more
         level = l * rank_part + lax.broadcasted_iota(jnp.int32, values.shape, 0)
         cbuf[p, ch] = jnp.where(level < ranks[0, 0], values, 0.0).astype(BF16)
         for d in range(1, tiles):
@@ -134,14 +152,18 @@
                 c_send.at[p, ch, d - 1], c_recv.at[p, ch, d - 1], (t + d) % tiles, l,
             )
 
+    def row_block(p, ch, at):
+        if p == 0:
+            return center[ch, at] + jnp.dot(
+                near_v[order[at], :, 0 : 2 * shard], zbuf[0, ch], preferred_element_type=F32
+            )
+        return jnp.dot(near_v[order[at]], stack[ch], preferred_element_type=F32)
+
     def stage_c(p, ch):
-        z_wait(p, ch)
         for at in range(4):
-            value = center[ch, at] + jnp.dot(
-                near_v[order[at], :, 0 : 2 * shard], zbuf[p, ch], preferred_element_type=F32
-            )
+            value = row_block(p, ch, at)
             if at < 2:
-                osend[p, ch, at] = value.astype(BF16)
+                osend[p, ch, at] = value
                 flying["o", p, ch, at] = send(
                     osend.at[p, ch, at], orecv.at[p, ch, at],
                     o_send.at[p, ch, at], o_recv.at[p, ch, at], t, peer(1),
@@ -151,40 +173,70 @@
 
     def stage_d(p, ch):
         flying["o", p, ch, 0].wait_recv()
-        xsend[p, ch] = (kept[ch, 0] + orecv[p, ch, 0].astype(F32)).astype(BF16)
+        xsend[p, ch] = (kept[ch, 0] + orecv[p, ch, 0]).astype(BF16)
         flying["x", p, ch] = send(
             xsend.at[p, ch], xrecv.at[p, ch], x_send.at[p, ch], x_recv.at[p, ch], t, peer(2)
         )
         flying["o", p, ch, 1].wait_recv()
-        fin[ch] = kept[ch, 1] + orecv[p, ch, 1].astype(F32)
+        fin[ch] = kept[ch, 1] + orecv[p, ch, 1]
+
+    def stage_n(ch):
+        flying["x", 0, ch].wait_recv()
+        value = fin[ch] + xrecv[0, ch].astype(F32)
+        fin[ch] = value
+        w[1, ch] = value.astype(BF16)
+        z_start(1, ch)
+        stage_pc(1, ch)
 
     def stage_e(p, ch):
-        wanted = rows[0, 0]
-        chosen = jnp.where(wanted == t, cbuf[p, ch].astype(F32), 0.0)
+        blocks = [cbuf[p, ch].astype(F32)]
         for d in range(1, tiles):
             flying["c", p, ch, d].wait_recv()
-            source = (t + tiles - d) % tiles
-            chosen = jnp.where(wanted == source, crecv[p, ch, d - 1].astype(F32), chosen)
-        sbuf[p, ch] = chosen.astype(BF16)
+            blocks.append(crecv[p, ch, d - 1].astype(F32))
+
+        def chosen(wanted):
+            value = jnp.zeros(blocks[0].shape, F32)
+            for d in range(tiles):
+                value = jnp.where(wanted == (t + tiles - d) % tiles, blocks[d], value)
+            return value.astype(BF16)
+
+        if p == 0:
+            sbuf[ch, 0] = chosen(rows[0, 0])
+            for way in range(2):
+                sbuf[ch, 1 + way] = chosen(row_recv[way, 0:1, 0:width])
+            source, held = sbuf.at[ch], srecv.at[ch, l]
+        else:
+            sbuf2[ch] = chosen(rows[0, 0])
+            source, held = sbuf2.at[ch], srecv2.at[ch, l]
         for k in (1, 2, 3):
             flying["s", p, ch, k] = send(
-                sbuf.at[p, ch], srecv.at[p, ch, k - 1],
-                s_send.at[p, ch, k - 1], s_recv.at[p, ch, k - 1], t, peer(k),
-            )
-
-    def stage_f(p, ch):
-        parts = [sbuf[p, ch].astype(F32)]
-        for k in (1, 2, 3):
-            flying["s", p, ch, k].wait_recv()
-            parts.append(srecv[p, ch, k - 1].astype(F32))
-        coefficients = jnp.concatenate(parts, axis=0).astype(BF16)
+                source, held, s_send.at[p, ch, k - 1], s_recv.at[p, ch, k - 1], t, peer(k),
+            )
+        if p == 0:
+            srecv[ch, l] = sbuf[ch]
+        else:
+            srecv2[ch, l] = sbuf2[ch]
+
+    def stage_g(ch):
+        for k in (1, 2, 3):
+            flying["s", 0, ch, k].wait_recv()
+        of = [joined([srecv[ch, k, at] for k in range(4)]).astype(BF16) for at in range(3)]
+        stage_b(1, ch, jnp.dot(mix[...], of[0], preferred_element_type=F32))
+        far = jnp.dot(left_t[...], of[0], preferred_element_type=F32)
+        stack[ch, 2 * shard : 3 * shard] = (fin[ch] + far).astype(BF16)
+        flying["z", 1, ch].wait_recv()
+        for way in range(2):
+            far = jnp.dot(left_tn[way], of[1 + way], preferred_element_type=F32)
+            part = slice(way * shard, (way + 1) * shard)
+            stack[ch, part] = (zbuf[1, ch, part].astype(F32) + far).astype(BF16)
+
+    def stage_f(ch):
+        for k in (1, 2, 3):
+            flying["s", 1, ch, k].wait_recv()
+        coefficients = joined([srecv2[ch, k] for k in range(4)]).astype(BF16)
         far = fin[ch] + jnp.dot(left_t[...], coefficients, preferred_element_type=F32)
-        flying["x", p, ch].wait_recv()
-        value = far + xrecv[p, ch].astype(F32)
-        if p == 0:
-            w[1, ch] = value.astype(BF16)
-        else:
-            out[:, ch * width : (ch + 1) * width] = value
+        flying["x", 1, ch].wait_recv()
+        out[:, ch * width : (ch + 1) * width] = far + xrecv[1, ch].astype(F32)
 
     def bases(source, held, base):
         copies = []
@@ -192,10 +244,11 @@
             columns = pl.ds(pl.multiple_of(peer(k) * shard, shard), shard)
             copies.append(
                 send(
-                    source.at[:, columns], held.at[k],
+                    source.at[:, columns], held.at[l],
                     set_send.at[base + k], set_recv.at[base + k], t, peer(k),
                 )
             )
+        held[l] = source[:, own]
         return copies
 
     loads[0].wait()
@@ -204,51 +257,63 @@
         z_start(0, ch)
     loads[2].wait()
     left_copies = bases(left_v, left_x, 4)
+    row_copies = Both(row_send, lambda way: row_recv.at[way], side_send.at[0], side_recv.at[0]).start()
+    sent.append(row_copies)
+    loads[3].wait()
+    for ch in range(CHUNKS):
+        stage_center(ch)
     for copy in right_copies:
         copy.wait_recv()
-    right_c[...] = jnp.concatenate([right_v[:, own].astype(F32)] + [right_x[k].astype(F32) for k in (1, 2, 3)], axis=0).astype(BF16)
+    right_c[...] = joined([right_x[k] for k in range(4)]).astype(BF16)
     for ch in range(CHUNKS):
         stage_pc(0, ch)
-    loads[3].wait()
-    for ch in range(CHUNKS):
-        stage_center(0, ch)
+    for copy in left_copies:
+        copy.wait_recv()
+    beside = Both(left_x, lambda way: left_n.at[way], side_send.at[1], side_recv.at[1]).start()
+    sent.append(beside)
+    left_t[...] = joined([left_x[k] for k in range(4)]).T.astype(BF16)
     loads[4].wait()
     loads[5].wait()
-
-    for p in range(2):
-        stage_b(p, 0)
-        stage_c(p, 0)
-        stage_b(p, 1)
-        stage_c(p, 1)
-        if p == 0:
-            for copy in left_copies:
-                copy.wait_recv()
-            left_t[...] = (
-                jnp.concatenate([left_v[:, own].astype(F32)] + [left_x[k].astype(F32) for k in (1, 2, 3)], axis=0).T.astype(BF16)
-            )
-        stage_d(p, 0)
-        stage_e(p, 0)
-        stage_d(p, 1)
-        stage_e(p, 1)
-        for ch in range(CHUNKS):
-            stage_f(p, ch)
-            if p == 0:
-                z_start(1, ch)
-                stage_pc(1, ch)
-                stage_center(1, ch)
+    for ch in range(CHUNKS):
+        flying["z", 0, ch].wait_recv()
+        stage_c(0, ch)
+    stage_d(0, 0)
+    for ch in range(CHUNKS):
+        stage_b(0, ch)
+    stage_d(0, 1)
+
+    part = jnp.dot(right_c[...], left_t[...], preferred_element_type=F32)
+    for k in range(4):
+        mix_part[k] = part[k * rank_part : (k + 1) * rank_part]
+    mix_copies = [
+        send(mix_part.at[peer(k)], mix_recv.at[k - 1], set_send.at[8 + k], set_recv.at[8 + k], t, peer(k))
+        for k in (1, 2, 3)
+    ]
+    beside.wait_recv()
+    row_copies.wait_recv()
+    for way in range(2):
+        left_tn[way] = joined([left_n[way, k] for k in range(4)]).T.astype(BF16)
+
+    stage_n(0)
+    stage_e(0, 0)
+    stage_n(1)
+    stage_e(0, 1)
+    for copy in mix_copies:
+        copy.wait_recv()
+    mix[...] = (mix_part[l] + mix_recv[0] + mix_recv[1] + mix_recv[2]).astype(BF16)
+    stage_g(0)
+    stage_c(1, 0)
+    stage_g(1)
+    stage_d(1, 0)
+    stage_c(1, 1)
+    stage_d(1, 1)
+    stage_e(1, 0)
+    stage_e(1, 1)
+    for ch in range(CHUNKS):
+        stage_f(ch)
 
     for copy in sent:
         copy.wait_send()
-    for p in range(2):
-        for ch in range(CHUNKS):
-
-            @pl.when(t < tiles - 1)
-            def _():
-                z_copy(p, ch, 0).wait_send()
-
-            @pl.when(t > 0)
-            def _():
-                z_copy(p, ch, 1).wait_send()
 
 
 def fused(tiles, probes, right_bases, left_bases, near_tiles, tile_ranks, row_columns):
@@ -257,6 +322,7 @@
     width = probe_count // CHUNKS
     near = near_tiles[0].transpose(1, 0, 2).reshape(3, 4, shard, shard)
     both = (2, CHUNKS)
+    full = -(-4 * rank_part // 128) * 128
     any_spec = pl.BlockSpec(memory_space=pltpu.HBM)
     smem_spec = pl.BlockSpec(memory_space=pltpu.SMEM)
     dma = pltpu.SemaphoreType.DMA
@@ -272,14 +338,22 @@
             pltpu.VMEM((rank_part, 4 * shard), BF16),
             pltpu.VMEM((4, rank_part, shard), BF16),
             pltpu.VMEM((4, rank_part, shard), BF16),
-            pltpu.VMEM((4 * rank_part, shard), BF16),
-            pltpu.VMEM((shard, 4 * rank_part), BF16),
+            pltpu.VMEM((2, 4, rank_part, shard), BF16),
+            pltpu.VMEM((full, shard), BF16),
+            pltpu.VMEM((shard, full), BF16),
+            pltpu.VMEM((2, shard, full), BF16),
+            pltpu.VMEM((8, width), jnp.int32),
+            pltpu.VMEM((2, 8, width), jnp.int32),
+            pltpu.VMEM((4, rank_part, full), F32),
+            pltpu.VMEM((3, rank_part, full), F32),
+            pltpu.VMEM((rank_part, full), BF16),
             pltpu.VMEM(both + (shard, width), BF16),
             pltpu.VMEM(both + (2 * shard, width), BF16),
+            pltpu.VMEM((CHUNKS, 3 * shard, width), BF16),
             pltpu.VMEM((CHUNKS, 4, shard, width), F32),
             pltpu.VMEM((CHUNKS, 2, shard, width), F32),
-            pltpu.VMEM(both + (2, shard, width), BF16),
-            pltpu.VMEM(both + (2, shard, width), BF16),
+            pltpu.VMEM(both + (2, shard, width), F32),
+            pltpu.VMEM(both + (2, shard, width), F32),
             pltpu.VMEM(both + (shard, width), BF16),
             pltpu.VMEM(both + (shard, width), BF16),
             pltpu.VMEM((CHUNKS, shard, width), F32),
@@ -287,9 +361,11 @@
             pltpu.VMEM(both + (3, rank_part, width), BF16),
             pltpu.VMEM(both + (rank_part, width), BF16),
             pltpu.VMEM(both + (tiles - 1, rank_part, width), BF16),
-            pltpu.VMEM(both + (rank_part, width), BF16),
-            pltpu.VMEM(both + (3, rank_part, width), BF16),
-            dma((6,)), dma((8,)), dma((8,)), dma(both + (2,)), dma(both + (2,)),
+            pltpu.VMEM((CHUNKS, 3, rank_part, width), BF16),
+            pltpu.VMEM((CHUNKS, 4, 3, rank_part, width), BF16),
+            pltpu.VMEM((CHUNKS, rank_part, width), BF16),
+            pltpu.VMEM((CHUNKS, 4, rank_part, width), BF16),
+            dma((6,)), dma((12,)), dma((12,)), dma((2, 2)), dma((2, 2)), dma(both + (2,)), dma(both + (2,)),
             dma(both + (3,)), dma(both + (3,)), dma(both + (tiles - 1,)), dma(both + (tiles - 1,)),
             dma(both + (3,)), dma(both + (3,)), dma(both + (2,)), dma(both + (2,)),
             dma(both), dma(both),

time: 32.8 us -> 30.6 us (0.933)
  Pallas kernels: 29.7 us -> 27.5 us
    pallas_call x1, Pallas kernels: 29.7 us -> 27.5 us  [fused(): pl.pallas_call(functools.partial(fused_kernel, tiles), out_shape=jax.Shap...]
where the time goes in v1:
time: 30.6 us; the launch traced here: 30.5 us
  Pallas kernels  27.5 us (90%)
  local copies, waits for them, and re-layouts  1.67 us (5%)
  between operations  1.3 us (4%)
    pallas_call x1, Pallas kernels, fused(): pl.pallas_call(functools.partial(fused_kernel, tiles), out_shape=jax.Shap...  27.5 us
    unnamed x1, local copies, waits for them, and re-layouts  1.67 us

profile of v1, /device:TPU:0, one launch (start us, length us, event | category | flops | bytes accessed | tf_op | source)
XLA Modules:
  0.0 30.5 jit_solution(11058593621432057075)
XLA Ops:
  1.3 27.5 %shard_map.64 = f32[256,256]{1,0:T(8,128)} custom-call(bf16[3,4,256,256]{3,2,1,0:T(8,128)(2,1)} %bitcast.7, bf16[24,1024]{1,0:T(8,128)(2,1)} %bitcast.8, bf16[24,1024]{1,0:T(8,128)(2,1)} %bitcast.9, f32[256,256]{1,0:T(8,128)} %probes.1, s32[1,1]{1,0:T(1,128)S(6)} %copy.8.ranks, s32[1,1]{1,0:T(1,128)S(6)} %copy.9.rows), custom_call_target="tpu_custom_call" | custom-call | tf_op jit(solution)/shard_map/pallas_call | solution.py:329
  28.8 1.7 %copy.10 = f32[256,256]{1,0:T(8,128)} copy(f32[256,256]{1,0:T(8,128)} %shard_map.64) | data formatting | bytes 524288

commit v2 on v1

--- a/solution.py
+++ b/solution.py
@@ -328,7 +328,7 @@
     dma = pltpu.SemaphoreType.DMA
     return pl.pallas_call(
         functools.partial(fused_kernel, tiles),
-        out_shape=jax.ShapeDtypeStruct((shard, probe_count), F32),
+        out_shape=pltpu.VMEM((shard, probe_count), F32),
         in_specs=[any_spec] * 4 + [smem_spec] * 2,
         out_specs=pl.BlockSpec(memory_space=pltpu.VMEM),
         scratch_shapes=[
@@ -371,7 +371,7 @@
             dma(both), dma(both),
         ],
         compiler_params=pltpu.CompilerParams(
-            collective_id=0, has_side_effects=True, vmem_limit_bytes=67_043_328
+            collective_id=0, has_side_effects=True, vmem_limit_bytes=67_043_328 - 8 * shard * probe_count
         ),
     )(near, right_bases[0, 0], left_bases[0, 0], probes, tile_ranks, row_columns)
 

time: 30.6 us -> 29 us (0.948)
  local copies, waits for them, and re-layouts: 1.67 us -> 0.71 us
  Pallas kernels: 27.5 us -> 26.8 us
    unnamed x1, local copies, waits for them, and re-layouts: 1.67 us -> 0.71 us
    pallas_call x1, Pallas kernels: 27.5 us -> 26.8 us  [fused(): pl.pallas_call(functools.partial(fused_kernel, tiles), out_shape=pltpu.VM...]
where the time goes in v2:
time: 29 us; the launch traced here: 28.8 us
  Pallas kernels  26.8 us (92%)
  between operations  1.3 us (4%)
  local copies, waits for them, and re-layouts  0.71 us (2%)
    pallas_call x1, Pallas kernels, fused(): pl.pallas_call(functools.partial(fused_kernel, tiles), out_shape=pltpu.VM...  26.8 us
    unnamed x1, local copies, waits for them, and re-layouts  0.71 us

profile of v2, /device:TPU:0, one launch (start us, length us, event | category | flops | bytes accessed | tf_op | source)
XLA Modules:
  0.0 28.8 jit_solution(3900506709390989085)
XLA Ops:
  1.3 26.8 %shard_map.64 = f32[256,256]{1,0:T(8,128)S(1)} custom-call(bf16[3,4,256,256]{3,2,1,0:T(8,128)(2,1)} %bitcast.7, bf16[24,1024]{1,0:T(8,128)(2,1)} %bitcast.8, bf16[24,1024]{1,0:T(8,128)(2,1)} %bitcast.9, f32[256,256]{1,0:T(8,128)} %probes.1, s32[1,1]{1,0:T(1,128)S(6)} %copy.9.ranks, s32[1,1]{1,0:T(1,128)S(6)} %copy.10.rows), custom_call_target="tpu_custom_call" | custom-call | tf_op jit(solution)/shard_map/pallas_call | solution.py:329
  28.1 0.7 %copy.8 = f32[256,256]{1,0:T(8,128)} copy(f32[256,256]{1,0:T(8,128)S(1)} %shard_map.64) | data formatting | bytes 524288

commit v3 on v2

--- a/solution.py
+++ b/solution.py
@@ -20,8 +20,7 @@
     row_send, row_recv, mix_part, mix_recv, mix,
     w, zbuf, stack, center, kept, osend, orecv, xsend, xrecv, fin,
     pc, prec, cbuf, crecv, sbuf, srecv, sbuf2, srecv2,
-    local_sem, set_send, set_recv, side_send, side_recv, z_send, z_recv, p_send, p_recv,
-    c_send, c_recv, s_send, s_recv, o_send, o_recv, x_send, x_recv,
+    local_sem, send_sem, set_recv, side_recv, z_recv, p_recv, c_recv, s_recv, o_recv, x_recv,
 ):
     g, t, l = lax.axis_index("group"), lax.axis_index("tile"), lax.axis_index("list")
     x, c = l // 2, l % 2
@@ -74,9 +73,12 @@
 
     sent = []
 
-    def send(src, dst, ssem, rsem, tile, lst):
+    def arrive(held, sem):
+        pltpu.make_async_copy(held, held, sem).wait()
+
+    def send(src, dst, rsem, tile, lst):
         copy = pltpu.make_async_remote_copy(
-            src_ref=src, dst_ref=dst, send_sem=ssem, recv_sem=rsem,
+            src_ref=src, dst_ref=dst, send_sem=send_sem, recv_sem=rsem,
             device_id=(g, tile, lst), device_id_type=MESH,
         )
         copy.start()
@@ -84,10 +86,10 @@
         return copy
 
     class Both:
-        def __init__(self, src, dst, ssem, rsem):
+        def __init__(self, src, dst, rsem):
             self.copies = [
                 pltpu.make_async_remote_copy(
-                    src_ref=src, dst_ref=dst(way), send_sem=ssem.at[way], recv_sem=rsem.at[way],
+                    src_ref=src, dst_ref=dst(way), send_sem=send_sem, recv_sem=rsem.at[way],
                     device_id=(g, (t + (1 if way == 0 else tiles - 1)) % tiles, l),
                     device_id_type=MESH,
                 )
@@ -116,7 +118,7 @@
     def z_start(p, ch):
         flying["z", p, ch] = Both(
             w.at[p, ch], lambda way: zbuf.at[p, ch, pl.ds(way * shard, shard)],
-            z_send.at[p, ch], z_recv.at[p, ch],
+            z_recv.at[p, ch],
         ).start()
         sent.append(flying["z", p, ch])
 
@@ -127,10 +129,7 @@
         for k in range(4):
             pc[p, ch, k] = values[k * rank_part : (k + 1) * rank_part].astype(BF16)
         for k in (1, 2, 3):
-            flying["p", p, ch, k] = send(
-                pc.at[p, ch, peer(k)], prec.at[p, ch, k - 1],
-                p_send.at[p, ch, k - 1], p_recv.at[p, ch, k - 1], t, peer(k),
-            )
+            send(pc.at[p, ch, peer(k)], prec.at[p, ch, k - 1], p_recv.at[p, ch], t, peer(k))
 
     def stage_center(ch):
         for at in range(4):
@@ -139,18 +138,14 @@
             )
 
     def stage_b(p, ch, more=None):
-        for k in (1, 2, 3):
-            flying["p", p, ch, k].wait_recv()
+        arrive(prec.at[p, ch], p_recv.at[p, ch])
         values = sum(prec[p, ch, k].astype(F32) for k in range(3)) + pc[p, ch, l].astype(F32)
         if more is not None:
             values = values + more
         level = l * rank_part + lax.broadcasted_iota(jnp.int32, values.shape, 0)
         cbuf[p, ch] = jnp.where(level < ranks[0, 0], values, 0.0).astype(BF16)
         for d in range(1, tiles):
-            flying["c", p, ch, d] = send(
-                cbuf.at[p, ch], crecv.at[p, ch, d - 1],
-                c_send.at[p, ch, d - 1], c_recv.at[p, ch, d - 1], (t + d) % tiles, l,
-            )
+            send(cbuf.at[p, ch], crecv.at[p, ch, d - 1], c_recv.at[p, ch], (t + d) % tiles, l)
 
     def row_block(p, ch, at):
         if p == 0:
@@ -165,8 +160,7 @@
             if at < 2:
                 osend[p, ch, at] = value
                 flying["o", p, ch, at] = send(
-                    osend.at[p, ch, at], orecv.at[p, ch, at],
-                    o_send.at[p, ch, at], o_recv.at[p, ch, at], t, peer(1),
+                    osend.at[p, ch, at], orecv.at[p, ch, at], o_recv.at[p, ch, at], t, peer(1)
                 )
             else:
                 kept[ch, at - 2] = value
@@ -175,7 +169,7 @@
         flying["o", p, ch, 0].wait_recv()
         xsend[p, ch] = (kept[ch, 0] + orecv[p, ch, 0]).astype(BF16)
         flying["x", p, ch] = send(
-            xsend.at[p, ch], xrecv.at[p, ch], x_send.at[p, ch], x_recv.at[p, ch], t, peer(2)
+            xsend.at[p, ch], xrecv.at[p, ch], x_recv.at[p, ch], t, peer(2)
         )
         flying["o", p, ch, 1].wait_recv()
         fin[ch] = kept[ch, 1] + orecv[p, ch, 1]
@@ -189,9 +183,9 @@
         stage_pc(1, ch)
 
     def stage_e(p, ch):
+        arrive(crecv.at[p, ch], c_recv.at[p, ch])
         blocks = [cbuf[p, ch].astype(F32)]
         for d in range(1, tiles):
-            flying["c", p, ch, d].wait_recv()
             blocks.append(crecv[p, ch, d - 1].astype(F32))
 
         def chosen(wanted):
@@ -209,17 +203,14 @@
             sbuf2[ch] = chosen(rows[0, 0])
             source, held = sbuf2.at[ch], srecv2.at[ch, l]
         for k in (1, 2, 3):
-            flying["s", p, ch, k] = send(
-                source, held, s_send.at[p, ch, k - 1], s_recv.at[p, ch, k - 1], t, peer(k),
-            )
+            send(source, held, s_recv.at[p, ch], t, peer(k))
         if p == 0:
             srecv[ch, l] = sbuf[ch]
         else:
             srecv2[ch, l] = sbuf2[ch]
 
     def stage_g(ch):
-        for k in (1, 2, 3):
-            flying["s", 0, ch, k].wait_recv()
+        arrive(srecv.at[ch, pl.ds(0, 3)], s_recv.at[0, ch])
         of = [joined([srecv[ch, k, at] for k in range(4)]).astype(BF16) for at in range(3)]
         stage_b(1, ch, jnp.dot(mix[...], of[0], preferred_element_type=F32))
         far = jnp.dot(left_t[...], of[0], preferred_element_type=F32)
@@ -231,45 +222,35 @@
             stack[ch, part] = (zbuf[1, ch, part].astype(F32) + far).astype(BF16)
 
     def stage_f(ch):
-        for k in (1, 2, 3):
-            flying["s", 1, ch, k].wait_recv()
+        arrive(srecv2.at[ch, pl.ds(0, 3)], s_recv.at[1, ch])
         coefficients = joined([srecv2[ch, k] for k in range(4)]).astype(BF16)
         far = fin[ch] + jnp.dot(left_t[...], coefficients, preferred_element_type=F32)
         flying["x", 1, ch].wait_recv()
         out[:, ch * width : (ch + 1) * width] = far + xrecv[1, ch].astype(F32)
 
-    def bases(source, held, base):
-        copies = []
+    def bases(source, held, at):
         for k in (1, 2, 3):
             columns = pl.ds(pl.multiple_of(peer(k) * shard, shard), shard)
-            copies.append(
-                send(
-                    source.at[:, columns], held.at[l],
-                    set_send.at[base + k], set_recv.at[base + k], t, peer(k),
-                )
-            )
+            send(source.at[:, columns], held.at[l], set_recv.at[at], t, peer(k))
         held[l] = source[:, own]
-        return copies
 
     loads[0].wait()
-    right_copies = bases(right_v, right_x, 0)
+    bases(right_v, right_x, 0)
     for ch in range(CHUNKS):
         z_start(0, ch)
     loads[2].wait()
-    left_copies = bases(left_v, left_x, 4)
-    row_copies = Both(row_send, lambda way: row_recv.at[way], side_send.at[0], side_recv.at[0]).start()
+    bases(left_v, left_x, 1)
+    row_copies = Both(row_send, lambda way: row_recv.at[way], side_recv.at[0]).start()
     sent.append(row_copies)
     loads[3].wait()
     for ch in range(CHUNKS):
         stage_center(ch)
-    for copy in right_copies:
-        copy.wait_recv()
+    arrive(right_x.at[pl.ds(0, 3)], set_recv.at[0])
     right_c[...] = joined([right_x[k] for k in range(4)]).astype(BF16)
     for ch in range(CHUNKS):
         stage_pc(0, ch)
-    for copy in left_copies:
-        copy.wait_recv()
-    beside = Both(left_x, lambda way: left_n.at[way], side_send.at[1], side_recv.at[1]).start()
+    arrive(left_x.at[pl.ds(0, 3)], set_recv.at[1])
+    beside = Both(left_x, lambda way: left_n.at[way], side_recv.at[1]).start()
     sent.append(beside)
     left_t[...] = joined([left_x[k] for k in range(4)]).T.astype(BF16)
     loads[4].wait()
@@ -285,10 +266,8 @@
     part = jnp.dot(right_c[...], left_t[...], preferred_element_type=F32)
     for k in range(4):
         mix_part[k] = part[k * rank_part : (k + 1) * rank_part]
-    mix_copies = [
-        send(mix_part.at[peer(k)], mix_recv.at[k - 1], set_send.at[8 + k], set_recv.at[8 + k], t, peer(k))
-        for k in (1, 2, 3)
-    ]
+    for k in (1, 2, 3):
+        send(mix_part.at[peer(k)], mix_recv.at[k - 1], set_recv.at[2], t, peer(k))
     beside.wait_recv()
     row_copies.wait_recv()
     for way in range(2):
@@ -298,16 +277,15 @@
     stage_e(0, 0)
     stage_n(1)
     stage_e(0, 1)
-    for copy in mix_copies:
-        copy.wait_recv()
+    arrive(mix_recv, set_recv.at[2])
     mix[...] = (mix_part[l] + mix_recv[0] + mix_recv[1] + mix_recv[2]).astype(BF16)
     stage_g(0)
     stage_c(1, 0)
     stage_g(1)
     stage_d(1, 0)
     stage_c(1, 1)
+    stage_e(1, 0)
     stage_d(1, 1)
-    stage_e(1, 0)
     stage_e(1, 1)
     for ch in range(CHUNKS):
         stage_f(ch)
@@ -365,10 +343,8 @@
             pltpu.VMEM((CHUNKS, 4, 3, rank_part, width), BF16),
             pltpu.VMEM((CHUNKS, rank_part, width), BF16),
             pltpu.VMEM((CHUNKS, 4, rank_part, width), BF16),
-            dma((6,)), dma((12,)), dma((12,)), dma((2, 2)), dma((2, 2)), dma(both + (2,)), dma(both + (2,)),
-            dma(both + (3,)), dma(both + (3,)), dma(both + (tiles - 1,)), dma(both + (tiles - 1,)),
-            dma(both + (3,)), dma(both + (3,)), dma(both + (2,)), dma(both + (2,)),
-            dma(both), dma(both),
+            dma((6,)), dma, dma((3,)), dma((2, 2)), dma(both + (2,)), dma(both), dma(both), dma(both),
+            dma(both + (2,)), dma(both),
         ],
         compiler_params=pltpu.CompilerParams(
             collective_id=0, has_side_effects=True, vmem_limit_bytes=67_043_328 - 8 * shard * probe_count

time: 29 us -> 27.9 us (0.962)
  Pallas kernels: 26.8 us -> 25.8 us
    pallas_call x1, Pallas kernels: 26.8 us -> 25.8 us  [fused(): pl.pallas_call(functools.partial(fused_kernel, tiles), out_shape=pltpu.VM...]
where the time goes in v3:
time: 27.9 us; the launch traced here: 27.8 us
  Pallas kernels  25.8 us (92%)
  between operations  1.3 us (5%)
  local copies, waits for them, and re-layouts  0.71 us (3%)
    pallas_call x1, Pallas kernels, fused(): pl.pallas_call(functools.partial(fused_kernel, tiles), out_shape=pltpu.VM...  25.8 us
    unnamed x1, local copies, waits for them, and re-layouts  0.71 us

profile of v3, /device:TPU:0, one launch (start us, length us, event | category | flops | bytes accessed | tf_op | source)
XLA Modules:
  0.0 27.8 jit_solution(6967197642666855278)
XLA Ops:
  1.3 25.8 %shard_map.64 = f32[256,256]{1,0:T(8,128)S(1)} custom-call(bf16[3,4,256,256]{3,2,1,0:T(8,128)(2,1)} %bitcast.7, bf16[24,1024]{1,0:T(8,128)(2,1)} %bitcast.8, bf16[24,1024]{1,0:T(8,128)(2,1)} %bitcast.9, f32[256,256]{1,0:T(8,128)} %probes.1, s32[1,1]{1,0:T(1,128)S(6)} %copy.9.ranks, s32[1,1]{1,0:T(1,128)S(6)} %copy.10.rows), custom_call_target="tpu_custom_call" | custom-call | tf_op jit(solution)/shard_map/pallas_call | solution.py:307
  27.1 0.7 %copy.8 = f32[256,256]{1,0:T(8,128)} copy(f32[256,256]{1,0:T(8,128)S(1)} %shard_map.64) | data formatting | bytes 524288

commit v4 on v3

--- a/solution.py
+++ b/solution.py
@@ -18,7 +18,7 @@
     tiles, near, right, left, probes, ranks, rows, out,
     near_v, probe_v, right_v, left_v, right_x, left_x, left_n, right_c, left_t, left_tn,
     row_send, row_recv, mix_part, mix_recv, mix,
-    w, zbuf, stack, center, kept, osend, orecv, xsend, xrecv, fin,
+    w, zbuf, stack, center, kept, osend, orecv, osend2, orecv2, xsend, xrecv, fin,
     pc, prec, cbuf, crecv, sbuf, srecv, sbuf2, srecv2,
     local_sem, send_sem, set_recv, side_recv, z_recv, p_recv, c_recv, s_recv, o_recv, x_recv,
 ):
@@ -154,25 +154,29 @@
             )
         return jnp.dot(near_v[order[at]], stack[ch], preferred_element_type=F32)
 
-    def stage_c(p, ch):
+    def stage_c(p, ch, between=None):
         for at in range(4):
+            if at == 2 and between is not None:
+                between()
             value = row_block(p, ch, at)
             if at < 2:
-                osend[p, ch, at] = value
+                out_of, into = (osend, orecv) if p == 0 else (osend2, orecv2)
+                out_of[ch, at] = value.astype(out_of.dtype)
                 flying["o", p, ch, at] = send(
-                    osend.at[p, ch, at], orecv.at[p, ch, at], o_recv.at[p, ch, at], t, peer(1)
+                    out_of.at[ch, at], into.at[ch, at], o_recv.at[p, ch, at], t, peer(1)
                 )
             else:
                 kept[ch, at - 2] = value
 
     def stage_d(p, ch):
         flying["o", p, ch, 0].wait_recv()
-        xsend[p, ch] = (kept[ch, 0] + orecv[p, ch, 0]).astype(BF16)
+        into = orecv if p == 0 else orecv2
+        xsend[p, ch] = (kept[ch, 0] + into[ch, 0].astype(F32)).astype(BF16)
         flying["x", p, ch] = send(
             xsend.at[p, ch], xrecv.at[p, ch], x_recv.at[p, ch], t, peer(2)
         )
         flying["o", p, ch, 1].wait_recv()
-        fin[ch] = kept[ch, 1] + orecv[p, ch, 1]
+        fin[ch] = kept[ch, 1] + into[ch, 1].astype(F32)
 
     def stage_n(ch):
         flying["x", 0, ch].wait_recv()
@@ -209,10 +213,16 @@
         else:
             srecv2[ch, l] = sbuf2[ch]
 
+    chosen_of = {}
+
     def stage_g(ch):
         arrive(srecv.at[ch, pl.ds(0, 3)], s_recv.at[0, ch])
         of = [joined([srecv[ch, k, at] for k in range(4)]).astype(BF16) for at in range(3)]
         stage_b(1, ch, jnp.dot(mix[...], of[0], preferred_element_type=F32))
+        chosen_of[ch] = of
+
+    def stage_w(ch):
+        of = chosen_of[ch]
         far = jnp.dot(left_t[...], of[0], preferred_element_type=F32)
         stack[ch, 2 * shard : 3 * shard] = (fin[ch] + far).astype(BF16)
         flying["z", 1, ch].wait_recv()
@@ -280,8 +290,9 @@
     arrive(mix_recv, set_recv.at[2])
     mix[...] = (mix_part[l] + mix_recv[0] + mix_recv[1] + mix_recv[2]).astype(BF16)
     stage_g(0)
-    stage_c(1, 0)
-    stage_g(1)
+    stage_w(0)
+    stage_c(1, 0, lambda: stage_g(1))
+    stage_w(1)
     stage_d(1, 0)
     stage_c(1, 1)
     stage_e(1, 0)
@@ -330,8 +341,10 @@
             pltpu.VMEM((CHUNKS, 3 * shard, width), BF16),
             pltpu.VMEM((CHUNKS, 4, shard, width), F32),
             pltpu.VMEM((CHUNKS, 2, shard, width), F32),
-            pltpu.VMEM(both + (2, shard, width), F32),
-            pltpu.VMEM(both + (2, shard, width), F32),
+            pltpu.VMEM((CHUNKS, 2, shard, width), F32),
+            pltpu.VMEM((CHUNKS, 2, shard, width), F32),
+            pltpu.VMEM((CHUNKS, 2, shard, width), BF16),
+            pltpu.VMEM((CHUNKS, 2, shard, width), BF16),
             pltpu.VMEM(both + (shard, width), BF16),
             pltpu.VMEM(both + (shard, width), BF16),
             pltpu.VMEM((CHUNKS, shard, width), F32),

time: 27.9 us -> 27.6 us (0.989)
  Pallas kernels: 25.8 us -> 25.4 us
    pallas_call x1, Pallas kernels: 25.8 us -> 25.4 us  [fused(): pl.pallas_call(functools.partial(fused_kernel, tiles), out_shape=pltpu.VM...]
where the time goes in v4:
time: 27.6 us; the launch traced here: 27.4 us
  Pallas kernels  25.4 us (92%)
  between operations  1.3 us (5%)
  local copies, waits for them, and re-layouts  0.71 us (3%)
    pallas_call x1, Pallas kernels, fused(): pl.pallas_call(functools.partial(fused_kernel, tiles), out_shape=pltpu.VM...  25.4 us
    unnamed x1, local copies, waits for them, and re-layouts  0.71 us

profile of v4, /device:TPU:0, one launch (start us, length us, event | category | flops | bytes accessed | tf_op | source)
XLA Modules:
  0.0 27.4 jit_solution(1405254827595982587)
XLA Ops:
  1.3 25.4 %shard_map.64 = f32[256,256]{1,0:T(8,128)S(1)} custom-call(bf16[3,4,256,256]{3,2,1,0:T(8,128)(2,1)} %bitcast.7, bf16[24,1024]{1,0:T(8,128)(2,1)} %bitcast.8, bf16[24,1024]{1,0:T(8,128)(2,1)} %bitcast.9, f32[256,256]{1,0:T(8,128)} %probes.1, s32[1,1]{1,0:T(1,128)S(6)} %copy.9.ranks, s32[1,1]{1,0:T(1,128)S(6)} %copy.10.rows), custom_call_target="tpu_custom_call" | custom-call | tf_op jit(solution)/shard_map/pallas_call | solution.py:318
  26.7 0.7 %copy.8 = f32[256,256]{1,0:T(8,128)} copy(f32[256,256]{1,0:T(8,128)S(1)} %shard_map.64) | data formatting | bytes 524288
